TPU v7x, 512 devices: a whole 4x4x16 slice. The times are simulated.
512 devices in a mesh: slab: 128 (over x, z, core), sub: 4 (over y).
Axes of the slice: x: 4, y: 4, z: 16, core: 2. Of those that a mesh axis runs over, the one named last changes fastest.
Arguments:
- ensemble: float32 [2, 15, 80, 65536], P(None, None, None, ('slab', 'sub')), may hold values from -6 to 6
- obs_value: float32 [2, 256], replicated, may hold values from -6 to 6
- obs_var: float32 [2, 256], replicated, may hold values from 0.5 to 4
- obs_owner: int32 [2, 256, 1], replicated, may hold values from 0 to 127; in each aligned block of 256 rows (0 to 255, 256 to 511, ..., all dimensions but the last counted through in order) at most 8 rows name the same one
- obs_column: int32 [2, 256], replicated, may hold values from 0 to 511
- home_block: int32 [2, 256], replicated, may hold values from -1 to 1
- batch_order: int32 [2], replicated, may hold values from 0 to 1, each once
Outputs:
- analysis: float32 [2, 15, 80, 65536], P(None, None, None, ('slab', 'sub'))
- assimilated_priors: float32 [2, 256, 160], replicated
Inputs may be any that keep to these rules, and one draw needn't show every extreme that they name: `obs_owner`: in each batch no slab owns more than 8 observations; in some batch one slab owns exactly 8. `batch_order`: each batch appears once.
All inputs are finite; a program needn't handle non-finite values.
Results may differ from a plain program's by a relative error of at most 0.00012.
Values sent between devices are 32-bit elements; how exact they have to be, the bound alone decides.
A program may use at most 64 MiB of HBM per device.

v0:
```python
import jax
import jax.numpy as jnp
from jax import lax
from jax.sharding import PartitionSpec as P

BANDS = 2
BLK = 16
BATCHES = 2
CAP = 8
HIGHEST = lax.Precision.HIGHEST


def gc_weight(first, second, nblocks, length):
    block_gap = jnp.abs(first - second)
    block_gap = jnp.minimum(block_gap, nblocks - block_gap)
    scaled_gap = block_gap.astype(jnp.float32) / length
    near_part = (
        ((-0.25 * scaled_gap + 0.5) * scaled_gap + 0.625) * scaled_gap**3
        - 5.0 / 3.0 * scaled_gap**2
        + 1.0
    )
    floored = jnp.maximum(scaled_gap, 1.0)
    far_part = (
        (
            (((scaled_gap / 12.0 - 0.5) * scaled_gap + 0.625) * scaled_gap + 5.0 / 3.0) * scaled_gap
            - 5.0
        )
        * scaled_gap
        + 4.0
        - 2.0 / (3.0 * floored)
    )
    return jnp.where(scaled_gap <= 1.0, near_part, jnp.where(scaled_gap < 2.0, far_part, 0.0))


def obs_statistics(current, values, variances, members):
    banded = current.reshape(current.shape[0], BANDS, members)
    whole_obs = jnp.sum(banded, axis=1)
    centre = jnp.mean(whole_obs, axis=1, keepdims=True)
    spread = jnp.sum((whole_obs - centre) ** 2, axis=1) / (members - 1) + 1e-06
    post_var = 1.0 / (1.0 / spread + 1.0 / variances)
    post_mean = post_var * (centre[:, 0] / spread + values / variances)
    increments = (post_mean - centre[:, 0])[:, None] + (jnp.sqrt(post_var / spread) - 1.0)[
        :, None
    ] * (whole_obs - centre)
    deviations = banded - jnp.mean(banded, axis=2, keepdims=True)
    return (deviations, spread, increments)


def update_pool(pool, pool_homes, deviations, spread, increments, obs_homes, nblocks, decays):
    members = deviations.shape[2]
    banded = pool.reshape(pool.shape[0], BANDS, members)
    new_bands = []
    for band_no in range(BANDS):
        pool_band = banded[:, band_no, :]
        pool_dev = pool_band - jnp.mean(pool_band, axis=1, keepdims=True)
        weights = (
            gc_weight(pool_homes[:, None], obs_homes[None, :], nblocks, decays[band_no])
            / ((members - 1) * spread)[None, :]
        )
        crossed = jnp.einsum("pm,km->pk", pool_dev, deviations[:, band_no, :], precision=HIGHEST)
        change = jnp.einsum("pk,km->pm", crossed * weights, increments, precision=HIGHEST)
        new_bands.append(pool_band + change)
    return jnp.stack(new_bands, axis=1).reshape(pool.shape)


def update_state(
    ensemble, my_cols, deviations, spread, increments, obs_homes, valid, nblocks, decays
):
    members = ensemble.shape[2]
    new_bands = []
    for band_no in range(BANDS):
        band_layer = ensemble[band_no]
        layer_dev = band_layer - jnp.mean(band_layer, axis=1, keepdims=True)
        obs_dev = deviations[:, band_no, :]
        weights = (
            gc_weight((my_cols // BLK)[:, None], obs_homes[None, :], nblocks, decays[band_no])
            / ((members - 1) * spread)[None, :]
        )
        weights = jnp.where(valid[None, :], weights, 0.0)
        crossed = jnp.einsum("lmc,km->lck", layer_dev, obs_dev, precision=HIGHEST)
        change = jnp.einsum("lck,km->lmc", crossed * weights[None], increments, precision=HIGHEST)
        new_bands.append(band_layer + change)
    return jnp.stack(new_bands, axis=0)


def slot_table(owners, slot_rank, slab_number, capacity):
    obs_count = owners.shape[1]
    matches = (owners == slab_number)[:, None, :] & (
        slot_rank[:, None, :] == jnp.arange(capacity, dtype=jnp.int32)[None, :, None]
    )
    slot_obs = jnp.sum(
        jnp.where(matches, jnp.arange(obs_count, dtype=jnp.int32)[None, None, :], 0), axis=2
    )
    slot_valid = jnp.any(matches, axis=2)
    return (slot_obs, slot_valid)


def per_device(ensemble, obs_value, obs_var, obs_owner, obs_column, home_block, batch_order):
    members = ensemble.shape[2]
    levels_count = ensemble.shape[1]
    cols_dev = ensemble.shape[3]
    slab_count = lax.axis_size("slab")
    sub_count = lax.axis_size("sub")
    slab_index = lax.axis_index("slab")
    sub_index = lax.axis_index("sub")
    capacity = CAP
    cols_slab = cols_dev * sub_count
    nblocks = cols_slab * slab_count // BLK
    span_broad = cols_slab // (4 * BLK)
    span_narrow = max(span_broad // 4, 1)
    decays = (float(span_broad), float(span_narrow))
    assert 2 * span_broad + 1 <= cols_slab // BLK and slab_count >= 3
    owners = obs_owner[:, :, 0]
    obs_home = jnp.mod((owners * cols_slab + obs_column) // BLK + home_block, nblocks)
    onehot = (owners[:, :, None] == jnp.arange(slab_count, dtype=jnp.int32)[None, None, :]).astype(
        jnp.int32
    )
    running = jnp.cumsum(onehot, axis=1) - 1
    slot_rank = jnp.sum(onehot * running, axis=2)
    slot_global = owners * capacity + slot_rank
    slot_obs, slot_valid = slot_table(owners, slot_rank, slab_index, capacity)
    slot_column = jnp.take_along_axis(obs_column, slot_obs, axis=1)
    slot_level = slot_obs % levels_count
    holder = slot_column // cols_dev
    local_col = slot_column % cols_dev
    picked = ensemble[:, slot_level, :, local_col]
    retain = slot_valid & (holder == sub_index)
    picked = jnp.where(retain[:, :, None, None], picked, 0.0).reshape(
        BATCHES, capacity, BANDS * members
    )
    slab_slots = jnp.sum(lax.all_gather(picked, "sub", axis=0), axis=0)
    gathered = lax.all_gather(slab_slots, "slab", axis=1, tiled=True)
    priors = jnp.take_along_axis(gathered, slot_global[:, :, None], axis=1)
    first, second = (batch_order[0], batch_order[1])
    y0 = priors[first]
    stats0 = obs_statistics(y0, obs_value[first], obs_var[first], members)
    y1 = update_pool(priors[second], obs_home[second], *stats0, obs_home[first], nblocks, decays)
    stats1 = obs_statistics(y1, obs_value[second], obs_var[second], members)
    recorded = jnp.zeros_like(priors).at[first].set(y0).at[second].set(y1)
    my_cols = (slab_index * sub_count + sub_index) * cols_dev + jnp.arange(
        cols_dev, dtype=jnp.int32
    )
    near = [jnp.mod(slab_index + d, slab_count) for d in (-1, 0, 1)]
    for batch_id, stats in ((first, stats0), (second, stats1)):
        deviations, spread, increments = stats
        b_owners = lax.dynamic_index_in_dim(owners, batch_id, keepdims=True)
        b_rank = lax.dynamic_index_in_dim(slot_rank, batch_id, keepdims=True)
        tables = [slot_table(b_owners, b_rank, n, capacity) for n in near]
        idx = jnp.concatenate([t[0][0] for t in tables])
        valid = jnp.concatenate([t[1][0] for t in tables])
        ensemble = update_state(
            ensemble,
            my_cols,
            deviations[idx],
            spread[idx],
            increments[idx],
            obs_home[batch_id][idx],
            valid,
            nblocks,
            decays,
        )
    return (ensemble, recorded)


def solution(mesh):
    placed = (P(None, None, None, ("slab", "sub")), P(), P(), P(), P(), P(), P())
    return jax.shard_map(
        per_device,
        mesh=mesh,
        in_specs=placed,
        out_specs=(P(None, None, None, ("slab", "sub")), P()),
        check_vma=False,
    )
```

profile of v0, /device:TPU:1, one launch (start us, length us, event | category | flops | bytes accessed | tf_op | source)
XLA Modules:
  0.0 194.4 jit_solution(9131951338326680747)
XLA Ops:
  7.2 0.7 copy.71
  7.9 0.7 broadcast_compare_fusion
  8.6 0.8 copy.45
  9.4 0.4 fusion.29
  10.1 0.2 fusion.30
  10.3 0.2 select_reduce_fusion
  10.5 0.2 fusion.42
  10.7 0.7 gather_fusion.9
  11.7 1.0 copy.47
  12.8 0.6 gather_fusion
  13.6 10.3 %all_gather.6 = f32[4,2,8,160]{3,2,1,0:T(8,128)S(1)} all-gather(f32[1,2,8,160]{3,2,1,0:T(8,128)S(1)} %broadcast_select_fusion.1), channel_id=1, replica_groups=mesh['slab'=128,'sub'=4] {'sub'}, dimensions={0}, use_global_device_ids=true | all-gather | bytes 51200 | tf_op jit(solution)/shard_map/all_gather | solution.py:131
  23.9 0.6 reduce_sum.213
  24.6 0.6 fusion.104
  29.1 0.2 select_reduce_fusion.6
  29.2 0.2 select_reduce_fusion.3
  29.5 0.7 gather_fusion.3
  30.2 0.7 gather_fusion.7
  31.0 0.2 fusion.76
  31.4 0.7 and_reduce_fusion
  32.2 132.7 %all-gather.2.cloned.1.call-done = f32[2,1024,160]{2,1,0:T(8,128)} async-done(((f32[2,8,160]{2,1,0:T(8,128)}), f32[2,1024,160]{2,1,0:T(8,128)}) %all-gather.2.cloned.1.call-update) | async-done | bytes 1310736 | tf_op jit(solution)/shard_map/all_gather | solution.py:132
  164.9 6.2 %gather_fusion.10 = f32[512,160]{1,0:T(8,128)S(1)} fusion(f32[2,1024,160]{2,1,0:T(8,128)} %all-gather.2.cloned.1.call-done, s32[512]{0:T(512)S(1)} %bitcast.158), kind=kCustom, calls=%fused_computation.10 | custom fusion | bytes 659456 | tf_op jit(solution)/shard_map/jit(take_along_axis)/gather | solution.py:133
  171.1 0.2 copy.48
  171.4 0.7 select_dynamic-update-slice_fusion
  172.4 0.3 broadcast_subtract_fusion
  172.7 0.2 fusion.101
  172.9 0.6 gather_fusion.2
  173.7 0.2 multiply_reduce_fusion
  173.9 0.2 multiply_add_fusion
  174.1 0.6 gather_fusion.1
  174.7 0.8 convolution_multiply_fusion
  175.4 0.4 convolution_add_fusion
  175.8 0.7 gather_fusion.4
  176.5 0.8 convolution_multiply_fusion.1
  177.3 0.4 fusion.100
  177.8 0.7 gather_fusion.8
  178.7 0.5 convolution_multiply_fusion.5
  179.2 0.7 fusion.106
  180.1 0.6 gather_fusion.6
  180.8 0.6 gather_fusion.5
  181.4 0.5 convolution_multiply_fusion.3
  181.9 0.7 fusion.105
  182.6 0.5 convolution_multiply_fusion.4
  183.1 0.7 fusion.4
  183.8 0.5 convolution_multiply_fusion.2
  184.3 0.7 fusion.1
  185.0 1.2 pad_maximum_fusion
  186.2 0.6 constant_dynamic-update-slice_fusion
  186.8 0.7 copy-done.2
  (77 shorter events, 2.4 us)
Async XLA Ops:
  7.2 3.6 %copy-start = (s32[2,256]{1,0:T(2,128)S(1)}, s32[2,256]{1,0:T(2,128)}, u32[]{:S(2)}) copy-start(s32[2,256]{1,0:T(2,128)} %param.15) | copy-start | bytes 6148
  7.2 157.8 %all-gather.2.cloned.1.call-start = ((), (), s32[]{:S(2)}) async-start(), calls=%async_computation | async-start | bytes 2113536 | tf_op jit(solution)/shard_map/all_gather | solution.py:132
  9.9 1.8 copy-start.1
  11.7 12.8 %copy-start.4 = (s32[2]{0:T(128)S(1)}, s32[2]{0:T(128)}, u32[]{:S(2)}) copy-start(s32[2]{0:T(128)} %param.17) | copy-start | bytes 28
  11.7 16.0 %copy-start.3 = (s32[2,256,1]{1,2,0:T(1,128)S(1)}, s32[2,256,1]{1,2,0:T(1,128)}, u32[]{:S(2)}) copy-start(s32[2,256,1]{1,2,0:T(1,128)} %param.14) | copy-start | bytes 6148
  11.7 17.8 %copy-start.5 = (s32[2,256]{1,0:T(2,128)S(1)}, s32[2,256]{1,0:T(2,128)}, u32[]{:S(2)}) copy-start(s32[2,256]{1,0:T(2,128)} %param.16) | copy-start | bytes 6148
  12.8 18.6 %copy-start.6 = (f32[2,256]{1,0:T(2,128)S(1)}, f32[2,256]{1,0:T(2,128)}, u32[]{:S(2)}) copy-start(f32[2,256]{1,0:T(2,128)} %param.12) | copy-start | bytes 6148
  12.8 18.5 %copy-start.7 = (f32[2,256]{1,0:T(2,128)S(1)}, f32[2,256]{1,0:T(2,128)}, u32[]{:S(2)}) copy-start(f32[2,256]{1,0:T(2,128)} %param.13) | copy-start | bytes 6148
  12.8 18.6 %copy-start.8 = (s32[3]{0:T(128)S(1)}, s32[3]{0:T(128)}, u32[]{:S(2)}) copy-start(s32[3]{0:T(128)} %constant.306.clone.1) | copy-start | bytes 40
  186.8 0.7 copy-start.2
Sparse Core Ops, SparseCore 0:
  24.7 140.2 all-gather.1
where the time goes:
time: 195 us; the launch traced here: 194 us
  waiting for transfers between devices  133 us (68%)
  between operations  18.4 us (9%)
  local copies, waits for them, and re-layouts  18 us (9%)
  blocking collectives  10.3 us (5%)
  other arithmetic  7.86 us (4%)
  matrix products  7.03 us (4%)
    all_gather x1, waiting for transfers between devices, per_device(): gathered = lax.all_gather(slab_slots, 'slab', axis=1, tiled=True)  133 us
    all_gather x1, blocking collectives, per_device(): slab_slots = jnp.sum(lax.all_gather(picked, 'sub', axis=0), axis=0)  10.3 us
    gather x2, local copies, waits for them, and re-layouts, per_device(): priors = jnp.take_along_axis(gathered, slot_global[:, :, None], axis=1)  6.32 us
  transfers between devices with their start and end apart: 1, of which 1 were waited for; matrix products, arithmetic and copies ran while one was open for 2% of the time, Pallas kernels for 0%

commit v1 on v0

--- a/solution.py
+++ b/solution.py
@@ -129,7 +129,9 @@
         BATCHES, capacity, BANDS * members
     )
     slab_slots = jnp.sum(lax.all_gather(picked, "sub", axis=0), axis=0)
-    gathered = lax.all_gather(slab_slots, "slab", axis=1, tiled=True)
+    gathered = jnp.concatenate(
+        lax.all_to_all(jnp.stack([slab_slots] * lax.axis_size("slab")), "slab", 0, 0), axis=1
+    )
     priors = jnp.take_along_axis(gathered, slot_global[:, :, None], axis=1)
     first, second = (batch_order[0], batch_order[1])
     y0 = priors[first]

time: 195 us -> 167 us (0.86)
  waiting for transfers between devices: 133 us -> 90.9 us
  starting transfers between devices: 0.04 us -> 23.1 us
  between operations: 18.4 us -> 5.12 us
  local copies, waits for them, and re-layouts: 18 us -> 22.6 us
    all_gather x1 -> x0, waiting for transfers between devices: 133 us -> none  [per_device(): gathered = lax.all_gather(slab_slots, 'slab', axis=1, tiled=True)]
    all_to_all x0 -> x1, waiting for transfers between devices: none -> 90.9 us  [per_device(): lax.all_to_all(jnp.stack([slab_slots] * lax.axis_size('slab')), 'slab', 0...]
    all_to_all x0 -> x1, starting transfers between devices: none -> 23.1 us  [per_device(): lax.all_to_all(jnp.stack([slab_slots] * lax.axis_size('slab')), 'slab', 0...]
where the time goes in v1:
time: 167 us; the launch traced here: 166 us
  waiting for transfers between devices  90.9 us (54%)
  starting transfers between devices  23.1 us (14%)
  local copies, waits for them, and re-layouts  22.6 us (14%)
  blocking collectives  10.3 us (6%)
  other arithmetic  7.38 us (4%)
  matrix products  7.01 us (4%)
  between operations  5.12 us (3%)
    all_to_all x1, waiting for transfers between devices, per_device(): lax.all_to_all(jnp.stack([slab_slots] * lax.axis_size('slab')), 'slab', 0...  90.9 us
    all_to_all x1, starting transfers between devices, per_device(): lax.all_to_all(jnp.stack([slab_slots] * lax.axis_size('slab')), 'slab', 0...  23.1 us
    all_gather x1, blocking collectives, per_device(): slab_slots = jnp.sum(lax.all_gather(picked, 'sub', axis=0), axis=0)  10.3 us
    gather x2, local copies, waits for them, and re-layouts, per_device(): priors = jnp.take_along_axis(gathered, slot_global[:, :, None], axis=1)  7.59 us
  transfers between devices with their start and end apart: 1, of which 1 were waited for; matrix products, arithmetic and copies ran while one was open for 2% of the time, Pallas kernels for 0%

profile of v1, /device:TPU:1, one launch (start us, length us, event | category | flops | bytes accessed | tf_op | source)
XLA Modules:
  0.0 166.3 jit_solution(6122889330911309577)
XLA Ops:
  0.6 0.7 copy.74
  1.3 0.7 broadcast_compare_fusion
  2.0 0.8 copy.46
  2.8 0.4 fusion.29
  3.5 0.2 fusion.30
  3.7 0.2 select_reduce_fusion
  4.2 0.7 gather_fusion.9
  5.1 1.0 copy.48
  6.2 0.6 gather_fusion
  7.0 10.3 %all_gather.3 = f32[4,2,8,160]{3,2,1,0:T(8,128)S(1)} all-gather(f32[1,2,8,160]{3,2,1,0:T(8,128)S(1)} %broadcast_select_fusion.1), channel_id=1, replica_groups=mesh['slab'=128,'sub'=4] {'sub'}, dimensions={0}, use_global_device_ids=true | all-gather | bytes 51200 | tf_op jit(solution)/shard_map/all_gather | solution.py:131
  17.3 1.6 stack.14
  18.8 23.1 %all-to-all-start = ((f32[128,2,8,160]{3,2,1,0:T(8,128)}), f32[128,2,8,160]{3,2,1,0:T(8,128)}, u32[]{:S(2)}, u32[]{:S(2)}) async-start(f32[128,2,8,160]{3,2,1,0:T(8,128)} %stack.14), calls=%async_computation | async-start | bytes 4194304 | tf_op jit(solution)/shard_map/all_to_all | solution.py:133
  42.0 0.6 fusion.104
  46.8 0.2 select_reduce_fusion.3
  47.0 0.7 gather_fusion.3
  47.8 0.7 gather_fusion.7
  48.5 0.2 fusion.76
  48.9 0.8 and_reduce_fusion
  49.8 90.9 %all-to-all-done = f32[128,2,8,160]{3,2,1,0:T(8,128)} async-done(((f32[128,2,8,160]{3,2,1,0:T(8,128)}), f32[128,2,8,160]{3,2,1,0:T(8,128)}, u32[]{:S(2)}, u32[]{:S(2)}) %all-to-all-start) | async-done | bytes 1310752 | tf_op jit(solution)/shard_map/all_to_all | solution.py:133
  140.7 1.7 %copy_bitcast_fusion = f32[2,1024,160]{2,1,0:T(8,128)S(1)} fusion(f32[128,2,8,160]{3,2,1,0:T(8,128)} %all-to-all-done), kind=kLoop, calls=%fused_computation.11 | loop fusion | bytes 2621440 | tf_op jit(solution)/shard_map/reshape | solution.py:132
  142.4 6.4 %gather_fusion.10 = f32[512,160]{1,0:T(8,128)} fusion(f32[2,1024,160]{2,1,0:T(8,128)S(1)} %copy_bitcast_fusion, s32[512]{0:T(512)S(1)} %bitcast.163), kind=kCustom, calls=%fused_computation.10 | custom fusion | bytes 659456 | tf_op jit(solution)/shard_map/jit(take_along_axis)/gather | solution.py:135
  148.8 1.2 copy.50
  150.1 0.7 select_dynamic-update-slice_fusion
  151.2 0.3 broadcast_subtract_fusion
  151.5 0.2 fusion.101
  151.7 0.6 gather_fusion.2
  152.5 0.2 multiply_reduce_fusion
  152.7 0.2 multiply_add_fusion
  152.9 0.6 gather_fusion.1
  153.4 0.8 convolution_multiply_fusion
  154.2 0.4 convolution_add_fusion
  154.6 0.7 gather_fusion.4
  155.3 0.8 convolution_multiply_fusion.1
  156.1 0.4 fusion.100
  156.6 0.7 gather_fusion.8
  157.5 0.5 convolution_multiply_fusion.5
  158.0 0.7 fusion.106
  158.9 0.6 gather_fusion.6
  159.6 0.6 gather_fusion.5
  160.2 0.5 convolution_multiply_fusion.3
  160.7 0.7 fusion.105
  161.4 0.5 convolution_multiply_fusion.4
  161.9 0.7 fusion.4
  162.6 0.5 convolution_multiply_fusion.2
  163.1 0.7 fusion.1
  163.8 1.2 pad_maximum_fusion
  164.9 0.6 constant_dynamic-update-slice_fusion
  165.6 0.7 copy-done.2
  (78 shorter events, 2.6 us)
Async XLA Ops:
  0.6 3.5 %copy-start = (s32[2,256]{1,0:T(2,128)S(1)}, s32[2,256]{1,0:T(2,128)}, u32[]{:S(2)}) copy-start(s32[2,256]{1,0:T(2,128)} %param.15) | copy-start | bytes 6148
  3.3 1.8 %copy-start.1 = (f32[2,15,80,128]{3,2,1,0:T(8,128)S(1)}, f32[2,15,80,128]{3,2,1,0:T(8,128)}, u32[]{:S(2)}) copy-start(f32[2,15,80,128]{3,2,1,0:T(8,128)} %param.11) | copy-start | bytes 3686404
  18.8 23.1 %copy-start.4 = (s32[2]{0:T(128)S(1)}, s32[2]{0:T(128)}, u32[]{:S(2)}) copy-start(s32[2]{0:T(128)} %param.17) | copy-start | bytes 28
  18.8 26.3 %copy-start.3 = (s32[2,256,1]{1,2,0:T(1,128)S(1)}, s32[2,256,1]{1,2,0:T(1,128)}, u32[]{:S(2)}) copy-start(s32[2,256,1]{1,2,0:T(1,128)} %param.14) | copy-start | bytes 6148
  18.8 28.1 %copy-start.5 = (s32[2,256]{1,0:T(2,128)S(1)}, s32[2,256]{1,0:T(2,128)}, u32[]{:S(2)}) copy-start(s32[2,256]{1,0:T(2,128)} %param.16) | copy-start | bytes 6148
  18.8 121.8 %all-to-all-start = ((f32[128,2,8,160]{3,2,1,0:T(8,128)}), f32[128,2,8,160]{3,2,1,0:T(8,128)}, u32[]{:S(2)}, u32[]{:S(2)}) async-start(f32[128,2,8,160]{3,2,1,0:T(8,128)} %stack.14), calls=%async_computation | async-start | bytes 4194304 | tf_op jit(solution)/shard_map/all_to_all | solution.py:133
  41.9 6.9 %copy-start.6 = (f32[2,256]{1,0:T(2,128)S(1)}, f32[2,256]{1,0:T(2,128)}, u32[]{:S(2)}) copy-start(f32[2,256]{1,0:T(2,128)} %param.12) | copy-start | bytes 6148
  41.9 6.9 %copy-start.7 = (f32[2,256]{1,0:T(2,128)S(1)}, f32[2,256]{1,0:T(2,128)}, u32[]{:S(2)}) copy-start(f32[2,256]{1,0:T(2,128)} %param.13) | copy-start | bytes 6148
  41.9 6.9 %copy-start.8 = (s32[3]{0:T(128)S(1)}, s32[3]{0:T(128)}, u32[]{:S(2)}) copy-start(s32[3]{0:T(128)} %constant.306.clone.1) | copy-start | bytes 40
  165.6 0.7 copy-start.2
